TPU v7x, 32 devices: a whole 2x2x4 slice. The times are simulated.
32 devices in a mesh: groups: 2 (over x), seq: 16 (over z, y, core).
Axes of the slice: x: 2, y: 2, z: 4, core: 2. Of those that a mesh axis runs over, the one named last changes fastest.
Arguments:
- queries: bfloat16 [4096, 8192], P(('groups', 'seq')), parts along dimension 0, may hold values from -4.5 to 4.5
- keyvalue: bfloat16 [4096, 2048], P(('groups', 'seq')), parts along dimension 0, may hold values from -4.5 to 4.5
- doc_ids: int32 [4096], P(('groups', 'seq')), parts along dimension 0, may hold values from 0 to 7, never falling along the last dimension, each value on 1 to 512 neighbouring positions
- owner_tiles: int32 [32, 2], P(('groups', 'seq')), parts along dimension 0, may hold values from 0 to 15, as said below
- tile_counts: int32 [32], P(('groups', 'seq')), parts along dimension 0, may hold values from 0 to 2, as said below
Outputs:
- owned: bfloat16 [8192, 8192], P(('groups', 'seq')), parts along dimension 0
There are 2 independent parts, one for each index of `groups`. A program takes and returns all parts, laid end to end along the dimension named above; each array names one. Nothing has to cross between parts.
Inputs may be any that keep to these rules, and one draw needn't show every extreme that they name: `owner_tiles`: over the slots below each owner's count, every tile 0 to 15 is listed exactly once; the other slots hold 0. Tile t is listed either by its holder, the owner o with o * 128 <= t * 128 < (o + 1) * 128, or by the holder's partner, the owner whose index differs from the holder's by half the number of owners. `tile_counts`: the counts sum to 16; each is 0, 1 or 2, some owner has 2, and an owner has 2 exactly when its partner has 0.
All inputs are finite; a program needn't handle non-finite values.
Results may differ from a plain program's by a relative error of at most 0.0034.
Values may be sent and summed in bfloat16 or wider, within the bound.
A program may use at most 64 MiB of HBM per device.

v0:
```python
import jax
import jax.numpy as jnp
from jax import lax
from jax.sharding import PartitionSpec as P

QUERY_HEADS = 64
KEY_VALUE_HEADS = 8
HEAD_WIDTH = 128
TILE = 128
DOCUMENT_LIMIT = 512


def from_behind(shard, axis, by):
    count = lax.axis_size(axis)
    pairs = [(i, i + by) for i in range(count) if 0 <= i + by < count]
    return lax.ppermute(shard, axis, pairs)


def attend(queries, keys, value_rows, allowed):
    scale = queries.shape[-1] ** (-0.5)
    scores = jnp.einsum("rhgd,khd->hgrk", queries, keys, preferred_element_type=jnp.float32) * scale
    scores = jnp.where(allowed[None, None], scores, -jnp.inf)
    row_top = jnp.max(scores, axis=3, keepdims=True)
    exponent = jnp.exp(scores - row_top)
    totals = jnp.sum(exponent, axis=3, keepdims=True)
    weights = exponent.astype(jnp.bfloat16)
    mixed_rows = jnp.einsum(
        "hgrk,khd->rhgd", weights, value_rows, preferred_element_type=jnp.float32
    )
    return (mixed_rows / jnp.transpose(totals, (2, 0, 1, 3))).astype(jnp.bfloat16)


def deliver_owners(head_rows, all_lists, owner_tiles, seq_count, width):
    slots_dev = owner_tiles.shape[1]
    slot_rows = slots_dev * TILE
    tile_rows = jnp.arange(TILE, dtype=jnp.int32)
    row_index = jnp.transpose(all_lists)[:, None, :] * TILE + tile_rows[None, :, None]
    send_rows = jnp.take(head_rows, row_index.reshape(slot_rows, seq_count), axis=0)
    received = lax.all_to_all(send_rows, "seq", split_axis=1, concat_axis=1, tiled=True)
    return received.reshape(slot_rows, width)


def local(queries, keyvalue, doc_ids, owner_tiles, tile_counts):
    seq_count = lax.axis_size("seq")
    token_per_holder = queries.shape[0]
    width = queries.shape[1]
    head_share = QUERY_HEADS // seq_count
    group_width = QUERY_HEADS // KEY_VALUE_HEADS
    head_cols = head_share * HEAD_WIDTH
    slots_dev = owner_tiles.shape[1]
    reach_devs = (DOCUMENT_LIMIT - 1) // token_per_holder + 1
    doc_marks = doc_ids + 1
    kv_parts = [keyvalue]
    mark_parts = [doc_marks]
    for shift_by in range(1, reach_devs + 1):
        far_kv, far_marks = from_behind((keyvalue, doc_marks), "seq", shift_by)
        kv_parts.insert(0, far_kv)
        mark_parts.insert(0, far_marks)
    kv_near = jnp.concatenate(kv_parts, axis=0)
    near_marks = jnp.concatenate(mark_parts, axis=0)
    near_rows = kv_near.shape[0]
    keyvalue_grouped = kv_near.reshape(near_rows, KEY_VALUE_HEADS, 2, HEAD_WIDTH)
    q_place = jnp.arange(token_per_holder, dtype=jnp.int32) + reach_devs * token_per_holder
    k_place = jnp.arange(near_rows, dtype=jnp.int32)
    allowed = (doc_marks[:, None] == near_marks[None, :]) & (k_place[None, :] <= q_place[:, None])
    local_out = attend(
        queries.reshape(token_per_holder, KEY_VALUE_HEADS, group_width, HEAD_WIDTH),
        keyvalue_grouped[:, :, 0],
        keyvalue_grouped[:, :, 1],
        allowed,
    )
    local_out = local_out.reshape(token_per_holder, width)
    all_lists = lax.all_gather(owner_tiles, "seq", axis=0, tiled=True)
    out_send = local_out.reshape(token_per_holder, seq_count, head_cols)
    head_rows = lax.all_to_all(out_send, "seq", split_axis=1, concat_axis=0, tiled=True).reshape(
        token_per_holder * seq_count, head_cols
    )
    owned = deliver_owners(head_rows, all_lists, owner_tiles, seq_count, width)
    live = jnp.repeat(jnp.arange(slots_dev, dtype=jnp.int32) < tile_counts[0], TILE)
    return jnp.where(live[:, None], owned, jnp.zeros((), jnp.bfloat16))


def solution(mesh):
    placed = (
        P(("groups", "seq"), None),
        P(("groups", "seq"), None),
        P(("groups", "seq")),
        P(("groups", "seq"), None),
        P(("groups", "seq")),
    )
    return jax.shard_map(
        local, mesh=mesh, in_specs=placed, out_specs=P(("groups", "seq"), None), check_vma=False
    )
```

profile of v0, /device:TPU:15, one launch (start us, length us, event | category | flops | bytes accessed | tf_op | source)
XLA Modules:
  0.0 285.1 jit_solution(12777522837619255446)
XLA Ops:
  0.7 3.2 %collective-permute-start.4 = (s32[128]{0:T(128)S(1)}, s32[128]{0:T(128)S(1)}, u32[]{:S(2)}, u32[]{:S(2)}) collective-permute-start(s32[128]{0:T(128)S(1)} %broadcast_add_fusion), channel_id=1, source_target_pairs={{0,4},{1,5},{2,6},{3,7},{4,8},{5,9},{6,10},{7,11},{8,12},{9,13},{1... | collective-permute-start | bytes 1544 | tf_op jit(solution)/shard_map/ppermute | solution.py:16
  3.9 4.0 %collective-permute-start.5 = (s32[128]{0:T(128)S(1)}, s32[128]{0:T(128)S(1)}, u32[]{:S(2)}, u32[]{:S(2)}) collective-permute-start(s32[128]{0:T(128)S(1)} %broadcast_add_fusion), channel_id=1, source_target_pairs={{0,3},{1,4},{2,5},{3,6},{4,7},{5,8},{6,9},{7,10},{8,11},{9,12},{10... | collective-permute-start | bytes 1544 | tf_op jit(solution)/shard_map/ppermute | solution.py:16
  8.0 1.9 collective-permute-start.6
  9.9 3.4 %collective-permute-start.7 = (s32[128]{0:T(128)S(1)}, s32[128]{0:T(128)S(1)}, u32[]{:S(2)}, u32[]{:S(2)}) collective-permute-start(s32[128]{0:T(128)S(1)} %broadcast_add_fusion), channel_id=1, source_target_pairs={{0,1},{1,2},{2,3},{3,4},{4,5},{5,6},{6,7},{7,8},{8,9},{9,10},{10,1... | collective-permute-start | bytes 1544 | tf_op jit(solution)/shard_map/ppermute | solution.py:16
  14.6 1.9 collective-permute-start
  16.6 2.2 copy.71
  22.7 2.2 collective-permute-start.3
  25.1 5.3 %collective-permute-done = bf16[128,2048]{0,1:T(8,128)(2,1)S(1)} collective-permute-done((bf16[128,2048]{0,1:T(8,128)(2,1)S(1)}, bf16[128,2048]{0,1:T(8,128)(2,1)S(1)}, u32[]{:S(2)}, u32[]{:S(2)}) %collective-permute-start) | collective-permute-done | bytes 524320 | tf_op jit(solution)/shard_map/ppermute | solution.py:16
  30.5 9.0 %collective-permute-done.1 = bf16[128,2048]{0,1:T(8,128)(2,1)S(1)} collective-permute-done((bf16[128,2048]{0,1:T(8,128)(2,1)S(1)}, bf16[128,2048]{0,1:T(8,128)(2,1)S(1)}, u32[]{:S(2)}, u32[]{:S(2)}) %collective-permute-start.1) | collective-permute-done | bytes 524320 | tf_op jit(solution)/shard_map/ppermute | solution.py:16
  39.6 10.8 %collective-permute-done.2 = bf16[128,2048]{0,1:T(8,128)(2,1)S(1)} collective-permute-done((bf16[128,2048]{0,1:T(8,128)(2,1)S(1)}, bf16[128,2048]{0,1:T(8,128)(2,1)S(1)}, u32[]{:S(2)}, u32[]{:S(2)}) %collective-permute-start.2) | collective-permute-done | bytes 524320 | tf_op jit(solution)/shard_map/ppermute | solution.py:16
  50.6 5.5 %collective-permute-done.3 = bf16[128,2048]{0,1:T(8,128)(2,1)S(1)} collective-permute-done((bf16[128,2048]{0,1:T(8,128)(2,1)S(1)}, bf16[128,2048]{0,1:T(8,128)(2,1)S(1)}, u32[]{:S(2)}, u32[]{:S(2)}) %collective-permute-start.3) | collective-permute-done | bytes 524320 | tf_op jit(solution)/shard_map/ppermute | solution.py:16
  57.8 5.9 %fusion.2 = (f32[8,8,128]{2,1,0:T(8,128)S(1)}, f32[8,640,128,8]{2,1,3,0:T(8,128)S(1)}) fusion(pred[128,640]{0,1:T(8,128)(4,1)S(1)} %fusion.11, bf16[128,8,8,128]{3,2,1,0:T(8,128)(2,1)S(1)} %bitcast.69, bf16[640,8,2,128]{0,3,2,1:T(8,128)(2,1)} %bitcast.71), kind=kOutput, calls=%fused_computation.5 | convolution fusion | flops 1357897728 | bytes 24494080 | tf_op jit(solution)/shard_map/rhgd,khd->hgrk/dot_general | solution.py:21
  63.8 5.7 %fusion = f32[8,8,128]{2,1,0:T(8,128)} fusion(f32[8,640,128,8]{2,1,3,0:T(8,128)S(1)} %get-tuple-element.6, f32[8,8,128]{2,1,0:T(8,128)S(1)} %get-tuple-element.5, pred[128,640]{0,1:T(8,128)(4,1)S(1)} %fusion.11), kind=kLoop, calls=%fused_computation.3 | loop fusion | flops 20963328 | bytes 21118976 | tf_op jit(solution)/shard_map/reduce_sum | solution.py:25
  69.5 7.8 %fusion.6 = bf16[128,8,8,128]{0,3,2,1:T(8,128)(2,1)} fusion(f32[8,640,128,8]{2,1,3,0:T(8,128)S(1)} %get-tuple-element.6, f32[8,8,128]{2,1,0:T(8,128)S(1)} %get-tuple-element.5, pred[128,640]{0,1:T(8,128)(4,1)} %copy-done.2, f32[128,8,8]{0,2,1:T(8,128)} %bitcast.76, bf16[640,8,2,128]{0,3,2,1:T(8,128)(2,1)} %bitcast.72), kind=kOutput, calls=%fused_computation.10 | convolution fusion | flops 1365245952 | bytes 24526848 | tf_op jit(solution)/shard_map/hgrk,khd->rhgd/dot_general | solution.py:27
  77.2 6.8 %all-to-all-start = ((bf16[128,16,512]{0,2,1:T(8,128)(2,1)}), bf16[128,16,512]{0,2,1:T(8,128)(2,1)S(1)}, u32[]{:S(2)}, u32[]{:S(2)}) async-start(bf16[128,16,512]{0,2,1:T(8,128)(2,1)} %bitcast.74), calls=%async_computation | async-start | bytes 4194304 | tf_op jit(solution)/shard_map/all_to_all | solution.py:75
  84.1 56.9 %all-gather = s32[16,1,2]{2,1,0:T(1,128)S(1)} all-gather(s32[1,1,2]{2,1,0:T(1,128)S(1)} %bitcast.77), channel_id=1, replica_groups=mesh['groups'=2,'seq'=16] {'seq'}, dimensions={0}, use_global_device_ids=true | all-gather | bytes 136 | tf_op jit(solution)/shard_map/all_gather | solution.py:73
  142.7 2.9 %copy.61 = bf16[16,128,1,512]{3,1,0,2:T(8,128)(2,1)S(1)} copy(bf16[16,128,1,512]{1,3,0,2:T(8,128)(2,1)} %bitcast.70) | data formatting | bytes 4194304 | tf_op jit(solution)/shard_map/all_to_all | solution.py:75
  145.5 17.3 %gather_fusion = bf16[4096,512]{1,0:T(8,128)(2,1)} fusion(bf16[2048,512]{1,0:T(8,128)(2,1)S(1)} %bitcast.67, s32[4096]{0:T(1024)S(1)} %broadcast_clamp_fusion), kind=kCustom, calls=%fused_computation | custom fusion | bytes 8404992 | tf_op jit(solution)/shard_map/jit(_take)/gather | solution.py:38
  162.9 7.5 %copy_select_fusion = bf16[256,16,512]{2,0,1:T(8,128)(2,1)} fusion(bf16[256,16,512]{2,1,0:T(8,128)(2,1)} %bitcast.68, pred[256,16]{0,1:T(8,128)(4,1)S(1)} %compare_and_fusion), kind=kLoop, calls=%fused_computation.11 | loop fusion | flops 2097152 | bytes 8392704 | tf_op jit(solution)/shard_map/jit(_take)/select_n | solution.py:38
  170.4 4.9 %all-to-all-start.1 = ((bf16[256,16,512]{2,0,1:T(8,128)(2,1)}), bf16[256,16,512]{2,0,1:T(8,128)(2,1)}, u32[]{:S(2)}, u32[]{:S(2)}) async-start(bf16[256,16,512]{2,0,1:T(8,128)(2,1)} %copy_select_fusion), calls=%async_computation.1 | async-start | bytes 8388608 | tf_op jit(solution)/shard_map/all_to_all | solution.py:39
  176.0 92.0 %all-to-all-done.1 = bf16[256,16,512]{2,0,1:T(8,128)(2,1)} async-done(((bf16[256,16,512]{2,0,1:T(8,128)(2,1)}), bf16[256,16,512]{2,0,1:T(8,128)(2,1)}, u32[]{:S(2)}, u32[]{:S(2)}) %all-to-all-start.1) | async-done | bytes 4194336 | tf_op jit(solution)/shard_map/all_to_all | solution.py:39
  268.0 6.4 %copy.63 = bf16[256,16,512]{0,2,1:T(8,128)(2,1)} copy(bf16[256,16,512]{2,0,1:T(8,128)(2,1)} %all-to-all-done.1) | data formatting | bytes 8388608 | tf_op jit(solution)/shard_map/all_to_all | solution.py:39
  274.4 4.4 %bitcast_select_fusion.1 = bf16[256,8192]{0,1:T(8,128)(2,1)} fusion(bf16[256,16,512]{0,2,1:T(8,128)(2,1)} %copy.63, pred[256]{0:T(512)(128)(4,1)S(1)} %broadcast_bitcast_fusion), kind=kLoop, calls=%fused_computation.8 | loop fusion | flops 2097152 | bytes 8388864 | tf_op jit(solution)/shard_map/jit(_where)/select_n | solution.py:80
  278.8 6.3 %copy.64 = bf16[256,8192]{1,0:T(8,128)(2,1)} copy(bf16[256,8192]{0,1:T(8,128)(2,1)} %bitcast_select_fusion.1) | data formatting | bytes 8388608 | tf_op jit(solution)/shard_map/jit(_where)/select_n | solution.py:80
  (43 shorter events, 9.9 us)
Async XLA Ops:
  0.0 24.9 %copy-start.4 = (s32[128]{0:T(128)S(1)}, s32[128]{0:T(128)}, u32[]{:S(2)}) copy-start(s32[128]{0:T(128)} %param.7) | copy-start | bytes 1540
  0.7 18.0 %collective-permute-start.4 = (s32[128]{0:T(128)S(1)}, s32[128]{0:T(128)S(1)}, u32[]{:S(2)}, u32[]{:S(2)}) collective-permute-start(s32[128]{0:T(128)S(1)} %broadcast_add_fusion), channel_id=1, source_target_pairs={{0,4},{1,5},{2,6},{3,7},{4,8},{5,9},{6,10},{7,11},{8,12},{9,13},{1... | collective-permute-start | bytes 1544 | tf_op jit(solution)/shard_map/ppermute | solution.py:16
  3.9 16.8 %collective-permute-start.5 = (s32[128]{0:T(128)S(1)}, s32[128]{0:T(128)S(1)}, u32[]{:S(2)}, u32[]{:S(2)}) collective-permute-start(s32[128]{0:T(128)S(1)} %broadcast_add_fusion), channel_id=1, source_target_pairs={{0,3},{1,4},{2,5},{3,6},{4,7},{5,8},{6,9},{7,10},{8,11},{9,12},{10... | collective-permute-start | bytes 1544 | tf_op jit(solution)/shard_map/ppermute | solution.py:16
  8.0 14.7 %collective-permute-start.6 = (s32[128]{0:T(128)S(1)}, s32[128]{0:T(128)S(1)}, u32[]{:S(2)}, u32[]{:S(2)}) collective-permute-start(s32[128]{0:T(128)S(1)} %broadcast_add_fusion), channel_id=1, source_target_pairs={{0,2},{1,3},{2,4},{3,5},{4,6},{5,7},{6,8},{7,9},{8,10},{9,11},{10,... | collective-permute-start | bytes 1544 | tf_op jit(solution)/shard_map/ppermute | solution.py:16
  9.9 15.0 %collective-permute-start.7 = (s32[128]{0:T(128)S(1)}, s32[128]{0:T(128)S(1)}, u32[]{:S(2)}, u32[]{:S(2)}) collective-permute-start(s32[128]{0:T(128)S(1)} %broadcast_add_fusion), channel_id=1, source_target_pairs={{0,1},{1,2},{2,3},{3,4},{4,5},{5,6},{6,7},{7,8},{8,9},{9,10},{10,1... | collective-permute-start | bytes 1544 | tf_op jit(solution)/shard_map/ppermute | solution.py:16
  14.6 15.8 %collective-permute-start = (bf16[128,2048]{0,1:T(8,128)(2,1)S(1)}, bf16[128,2048]{0,1:T(8,128)(2,1)S(1)}, u32[]{:S(2)}, u32[]{:S(2)}) collective-permute-start(bf16[128,2048]{0,1:T(8,128)(2,1)S(1)} %copy.52), channel_id=1, source_target_pairs={{0,4},{1,5},{2,6},{3,7},{4,8},{5,9},{6,10},{7,11},{8,12},{9,13},{1... | collective-permute-start | bytes 1572872 | tf_op jit(solution)/shard_map/ppermute | solution.py:16
  18.8 20.7 %collective-permute-start.1 = (bf16[128,2048]{0,1:T(8,128)(2,1)S(1)}, bf16[128,2048]{0,1:T(8,128)(2,1)S(1)}, u32[]{:S(2)}, u32[]{:S(2)}) collective-permute-start(bf16[128,2048]{0,1:T(8,128)(2,1)S(1)} %copy.52), channel_id=1, source_target_pairs={{0,3},{1,4},{2,5},{3,6},{4,7},{5,8},{6,9},{7,10},{8,11},{9,12},{10... | collective-permute-start | bytes 1572872 | tf_op jit(solution)/shard_map/ppermute | solution.py:16
  20.7 29.8 %collective-permute-start.2 = (bf16[128,2048]{0,1:T(8,128)(2,1)S(1)}, bf16[128,2048]{0,1:T(8,128)(2,1)S(1)}, u32[]{:S(2)}, u32[]{:S(2)}) collective-permute-start(bf16[128,2048]{0,1:T(8,128)(2,1)S(1)} %copy.52), channel_id=1, source_target_pairs={{0,2},{1,3},{2,4},{3,5},{4,6},{5,7},{6,8},{7,9},{8,10},{9,11},{10,... | collective-permute-start | bytes 1572872 | tf_op jit(solution)/shard_map/ppermute | solution.py:16
  22.7 33.4 %collective-permute-start.3 = (bf16[128,2048]{0,1:T(8,128)(2,1)S(1)}, bf16[128,2048]{0,1:T(8,128)(2,1)S(1)}, u32[]{:S(2)}, u32[]{:S(2)}) collective-permute-start(bf16[128,2048]{0,1:T(8,128)(2,1)S(1)} %copy.52), channel_id=1, source_target_pairs={{0,1},{1,2},{2,3},{3,4},{4,5},{5,6},{6,7},{7,8},{8,9},{9,10},{10,1... | collective-permute-start | bytes 1572872 | tf_op jit(solution)/shard_map/ppermute | solution.py:16
  25.1 38.7 %copy-start.2 = (pred[128,640]{0,1:T(8,128)(4,1)}, pred[128,640]{0,1:T(8,128)(4,1)S(1)}, u32[]{:S(2)}) copy-start(pred[128,640]{0,1:T(8,128)(4,1)S(1)} %fusion.11) | copy-start | bytes 245764
  56.3 1.5 copy-start.1
  77.2 6.8 %copy-start.3 = (s32[1,2]{1,0:T(1,128)S(1)}, s32[1,2]{1,0:T(1,128)}, u32[]{:S(2)}) copy-start(s32[1,2]{1,0:T(1,128)} %param.8) | copy-start | bytes 28
  77.2 64.1 %all-to-all-start = ((bf16[128,16,512]{0,2,1:T(8,128)(2,1)}), bf16[128,16,512]{0,2,1:T(8,128)(2,1)S(1)}, u32[]{:S(2)}, u32[]{:S(2)}) async-start(bf16[128,16,512]{0,2,1:T(8,128)(2,1)} %bitcast.74), calls=%async_computation | async-start | bytes 4194304 | tf_op jit(solution)/shard_map/all_to_all | solution.py:75
  141.4 1.3 copy-start
  170.4 97.6 %all-to-all-start.1 = ((bf16[256,16,512]{2,0,1:T(8,128)(2,1)}), bf16[256,16,512]{2,0,1:T(8,128)(2,1)}, u32[]{:S(2)}, u32[]{:S(2)}) async-start(bf16[256,16,512]{2,0,1:T(8,128)(2,1)} %copy_select_fusion), calls=%async_computation.1 | async-start | bytes 8388608 | tf_op jit(solution)/shard_map/all_to_all | solution.py:39
where the time goes:
time: 286 us; the launch traced here: 285 us
  waiting for transfers between devices  123 us (43%)
  blocking collectives  56.9 us (20%)
  local copies, waits for them, and re-layouts  40.1 us (14%)
  starting transfers between devices  32.2 us (11%)
  other arithmetic  18.6 us (7%)
  matrix products  13.7 us (5%)
    all_to_all x1, waiting for transfers between devices, deliver_owners(): lax.all_to_all(send_rows, 'seq', split_axis=1, concat_axis=1, tiled=True)  92 us
    all_gather x1, blocking collectives, local(): all_lists = lax.all_gather(owner_tiles, 'seq', axis=0, tiled=True)  56.9 us
    ppermute x8, waiting for transfers between devices, from_behind(): return lax.ppermute(shard, axis, pairs)  30.7 us
    ppermute x8, starting transfers between devices, from_behind(): return lax.ppermute(shard, axis, pairs)  20.5 us
    gather x1, local copies, waits for them, and re-layouts, deliver_owners(): jnp.take(head_rows, row_index.reshape(slot_rows, seq_count), axis=0)  17.3 us
    dot_general x1, matrix products, attend(): jnp.einsum('hgrk,khd->rhgd', weights, value_rows, preferred_element_type=...  7.78 us
    select_n x2, other arithmetic, deliver_owners(): jnp.take(head_rows, row_index.reshape(slot_rows, seq_count), axis=0)  7.62 us
    all_to_all x1, starting transfers between devices, local(): lax.all_to_all(out_send, 'seq', split_axis=1, concat_axis=0, tiled=True)  6.8 us
  transfers between devices with their start and end apart: 10, of which 5 were waited for; matrix products, arithmetic and copies ran while one was open for 2% of the time, Pallas kernels for 0%

commit v1 on v0

--- a/solution.py
+++ b/solution.py
@@ -70,7 +70,21 @@
         allowed,
     )
     local_out = local_out.reshape(token_per_holder, width)
-    all_lists = lax.all_gather(owner_tiles, "seq", axis=0, tiled=True)
+
+    def connect_the_map(chunk):
+        so_far_all = [chunk]
+        extent = lax.axis_size("seq")
+        for u in range(extent - 1):
+            so_far_all.append(
+                lax.ppermute(
+                    so_far_all[-1], "seq", [(i0, (i0 + 1) % extent) for i0 in range(extent)]
+                )
+            )
+        return jnp.roll(
+            jnp.concatenate(so_far_all[::-1], 0), (lax.axis_index("seq") + 1) * chunk.shape[0], 0
+        )
+
+    all_lists = connect_the_map(owner_tiles)
     out_send = local_out.reshape(token_per_holder, seq_count, head_cols)
     head_rows = lax.all_to_all(out_send, "seq", split_axis=1, concat_axis=0, tiled=True).reshape(
         token_per_holder * seq_count, head_cols

time: 286 us -> 348 us (1.22)
  starting transfers between devices: 32.2 us -> 96.8 us
  blocking collectives: 56.9 us -> 0 us
  waiting for transfers between devices: 123 us -> 176 us
    all_gather x1 -> x0, blocking collectives: 56.9 us -> none  [local(): all_lists = lax.all_gather(owner_tiles, 'seq', axis=0, tiled=True)]
    ppermute x0 -> x15, waiting for transfers between devices: none -> 53.8 us  [connect_the_map(): lax.ppermute(so_far_all[-1], 'seq', [(i0, (i0 + 1) % extent) for i0 in ra...]
    ppermute x0 -> x15, starting transfers between devices: none -> 46 us  [connect_the_map(): lax.ppermute(so_far_all[-1], 'seq', [(i0, (i0 + 1) % extent) for i0 in ra...]
    all_to_all x1, starting transfers between devices: 4.89 us -> 23.5 us  [deliver_owners(): lax.all_to_all(send_rows, 'seq', split_axis=1, concat_axis=1, tiled=True)]
  transfers between devices with their start and end apart: 10 -> 25, of which waited for: 5 -> 20; matrix products, arithmetic and copies ran while one was open for 2% -> 1% of each run, Pallas kernels for 0% -> 0%
where the time goes in v1:
time: 348 us; the launch traced here: 347 us
  waiting for transfers between devices  176 us (51%)
  starting transfers between devices  96.8 us (28%)
  local copies, waits for them, and re-layouts  40.3 us (12%)
  other arithmetic  18.8 us (5%)
  matrix products  13.7 us (4%)
    all_to_all x1, waiting for transfers between devices, deliver_owners(): lax.all_to_all(send_rows, 'seq', split_axis=1, concat_axis=1, tiled=True)  91.7 us
    ppermute x15, waiting for transfers between devices, connect_the_map(): lax.ppermute(so_far_all[-1], 'seq', [(i0, (i0 + 1) % extent) for i0 in ra...  53.8 us
    ppermute x15, starting transfers between devices, connect_the_map(): lax.ppermute(so_far_all[-1], 'seq', [(i0, (i0 + 1) % extent) for i0 in ra...  46 us
    ppermute x8, waiting for transfers between devices, from_behind(): return lax.ppermute(shard, axis, pairs)  30.7 us
    all_to_all x1, starting transfers between devices, deliver_owners(): lax.all_to_all(send_rows, 'seq', split_axis=1, concat_axis=1, tiled=True)  23.5 us
    ppermute x8, starting transfers between devices, from_behind(): return lax.ppermute(shard, axis, pairs)  20.5 us
    gather x1, local copies, waits for them, and re-layouts, deliver_owners(): jnp.take(head_rows, row_index.reshape(slot_rows, seq_count), axis=0)  17.3 us
    dot_general x1, matrix products, attend(): jnp.einsum('hgrk,khd->rhgd', weights, value_rows, preferred_element_type=...  7.79 us
  transfers between devices with their start and end apart: 25, of which 20 were waited for; matrix products, arithmetic and copies ran while one was open for 1% of the time, Pallas kernels for 0%

profile of v1, /device:TPU:15, one launch (start us, length us, event | category | flops | bytes accessed | tf_op | source)
XLA Modules:
  0.0 346.8 jit_solution(13325079592044438856)
XLA Ops:
  0.7 3.2 collective-permute-start.19
  3.9 4.0 %collective-permute-start.20 = (s32[128]{0:T(128)S(1)}, s32[128]{0:T(128)S(1)}, u32[]{:S(2)}, u32[]{:S(2)}) collective-permute-start(s32[128]{0:T(128)S(1)} %broadcast_add_fusion), channel_id=1, source_target_pairs={{0,3},{1,4},{2,5},{3,6},{4,7},{5,8},{6,9},{7,10},{8,11},{9,12},{10... | collective-permute-start | bytes 1544 | tf_op jit(solution)/shard_map/ppermute | solution.py:16
  9.9 3.4 collective-permute-start.22
  25.1 5.3 %collective-permute-done.15 = bf16[128,2048]{0,1:T(8,128)(2,1)S(1)} collective-permute-done((bf16[128,2048]{0,1:T(8,128)(2,1)S(1)}, bf16[128,2048]{0,1:T(8,128)(2,1)S(1)}, u32[]{:S(2)}, u32[]{:S(2)}) %collective-permute-start.15) | collective-permute-done | bytes 524320 | tf_op jit(solution)/shard_map/ppermute | solution.py:16
  30.5 9.0 %collective-permute-done.16 = bf16[128,2048]{0,1:T(8,128)(2,1)S(1)} collective-permute-done((bf16[128,2048]{0,1:T(8,128)(2,1)S(1)}, bf16[128,2048]{0,1:T(8,128)(2,1)S(1)}, u32[]{:S(2)}, u32[]{:S(2)}) %collective-permute-start.16) | collective-permute-done | bytes 524320 | tf_op jit(solution)/shard_map/ppermute | solution.py:16
  39.6 10.8 %collective-permute-done.17 = bf16[128,2048]{0,1:T(8,128)(2,1)S(1)} collective-permute-done((bf16[128,2048]{0,1:T(8,128)(2,1)S(1)}, bf16[128,2048]{0,1:T(8,128)(2,1)S(1)}, u32[]{:S(2)}, u32[]{:S(2)}) %collective-permute-start.17) | collective-permute-done | bytes 524320 | tf_op jit(solution)/shard_map/ppermute | solution.py:16
  50.6 5.5 %collective-permute-done.18 = bf16[128,2048]{0,1:T(8,128)(2,1)S(1)} collective-permute-done((bf16[128,2048]{0,1:T(8,128)(2,1)S(1)}, bf16[128,2048]{0,1:T(8,128)(2,1)S(1)}, u32[]{:S(2)}, u32[]{:S(2)}) %collective-permute-start.18) | collective-permute-done | bytes 524320 | tf_op jit(solution)/shard_map/ppermute | solution.py:16
  57.8 5.9 %fusion.2 = (f32[8,8,128]{2,1,0:T(8,128)S(1)}, f32[8,640,128,8]{2,1,3,0:T(8,128)S(1)}) fusion(pred[128,640]{0,1:T(8,128)(4,1)S(1)} %fusion.11, bf16[128,8,8,128]{3,2,1,0:T(8,128)(2,1)S(1)} %bitcast.66, bf16[640,8,2,128]{0,3,2,1:T(8,128)(2,1)} %bitcast.68), kind=kOutput, calls=%fused_computation.5 | convolution fusion | flops 1357897728 | bytes 24494080 | tf_op jit(solution)/shard_map/rhgd,khd->hgrk/dot_general | solution.py:21
  63.8 5.7 %fusion = f32[8,8,128]{2,1,0:T(8,128)} fusion(f32[8,640,128,8]{2,1,3,0:T(8,128)S(1)} %get-tuple-element.6, f32[8,8,128]{2,1,0:T(8,128)S(1)} %get-tuple-element.5, pred[128,640]{0,1:T(8,128)(4,1)S(1)} %fusion.11), kind=kLoop, calls=%fused_computation.3 | loop fusion | flops 20963328 | bytes 21118976 | tf_op jit(solution)/shard_map/reduce_sum | solution.py:25
  69.5 7.8 %fusion.6 = bf16[128,8,8,128]{0,3,2,1:T(8,128)(2,1)} fusion(f32[8,640,128,8]{2,1,3,0:T(8,128)S(1)} %get-tuple-element.6, f32[8,8,128]{2,1,0:T(8,128)S(1)} %get-tuple-element.5, pred[128,640]{0,1:T(8,128)(4,1)} %copy-done.2, f32[128,8,8]{0,2,1:T(8,128)} %bitcast.73, bf16[640,8,2,128]{0,3,2,1:T(8,128)(2,1)} %bitcast.69), kind=kOutput, calls=%fused_computation.10 | convolution fusion | flops 1365245952 | bytes 24526848 | tf_op jit(solution)/shard_map/hgrk,khd->rhgd/dot_general | solution.py:27
  77.3 6.8 %all-to-all-start = ((bf16[128,16,512]{0,2,1:T(8,128)(2,1)}), bf16[128,16,512]{0,2,1:T(8,128)(2,1)S(1)}, u32[]{:S(2)}, u32[]{:S(2)}) async-start(bf16[128,16,512]{0,2,1:T(8,128)(2,1)} %bitcast.71), calls=%async_computation | async-start | bytes 4194304 | tf_op jit(solution)/shard_map/all_to_all | solution.py:89
  85.6 43.7 %collective-permute-done = s32[1,2]{0,1:T(2,128)S(1)} collective-permute-done((s32[1,2]{0,1:T(2,128)S(1)}, s32[1,2]{0,1:T(2,128)S(1)}, u32[]{:S(2)}, u32[]{:S(2)}) %collective-permute-start) | collective-permute-done | bytes 40 | tf_op jit(solution)/shard_map/ppermute | solution.py:79
  129.3 3.3 collective-permute-start.1
  133.3 3.2 collective-permute-start.2
  145.0 3.2 collective-permute-start.5
  164.5 3.2 collective-permute-start.10
  180.1 3.2 collective-permute-start.14
  188.7 17.3 %gather_fusion = bf16[4096,512]{1,0:T(8,128)(2,1)} fusion(bf16[2048,512]{1,0:T(8,128)(2,1)S(1)} %bitcast.64, s32[4096]{0:T(1024)S(1)} %broadcast_clamp_fusion), kind=kCustom, calls=%fused_computation | custom fusion | bytes 8404992 | tf_op jit(solution)/shard_map/jit(_take)/gather | solution.py:38
  206.1 7.6 %copy_select_fusion = bf16[256,16,512]{2,0,1:T(8,128)(2,1)} fusion(bf16[256,16,512]{2,1,0:T(8,128)(2,1)} %bitcast.65, pred[256,16]{0,1:T(8,128)(4,1)S(1)} %compare_and_fusion), kind=kLoop, calls=%fused_computation.11 | loop fusion | flops 2097152 | bytes 8392704 | tf_op jit(solution)/shard_map/jit(_take)/select_n | solution.py:38
  213.6 23.5 %all-to-all-start.1 = ((bf16[256,16,512]{2,0,1:T(8,128)(2,1)}), bf16[256,16,512]{2,0,1:T(8,128)(2,1)}, u32[]{:S(2)}, u32[]{:S(2)}) async-start(bf16[256,16,512]{2,0,1:T(8,128)(2,1)} %copy_select_fusion), calls=%async_computation.1 | async-start | bytes 8388608 | tf_op jit(solution)/shard_map/all_to_all | solution.py:39
  237.9 91.7 %all-to-all-done.1 = bf16[256,16,512]{2,0,1:T(8,128)(2,1)} async-done(((bf16[256,16,512]{2,0,1:T(8,128)(2,1)}), bf16[256,16,512]{2,0,1:T(8,128)(2,1)}, u32[]{:S(2)}, u32[]{:S(2)}) %all-to-all-start.1) | async-done | bytes 4194336 | tf_op jit(solution)/shard_map/all_to_all | solution.py:39
  329.6 6.4 %copy.52 = bf16[256,16,512]{0,2,1:T(8,128)(2,1)} copy(bf16[256,16,512]{2,0,1:T(8,128)(2,1)} %all-to-all-done.1) | data formatting | bytes 8388608 | tf_op jit(solution)/shard_map/all_to_all | solution.py:39
  336.0 4.4 %bitcast_select_fusion.1 = bf16[256,8192]{0,1:T(8,128)(2,1)} fusion(bf16[256,16,512]{0,2,1:T(8,128)(2,1)} %copy.52, pred[256]{0:T(512)(128)(4,1)S(1)} %broadcast_bitcast_fusion), kind=kLoop, calls=%fused_computation.8 | loop fusion | flops 2097152 | bytes 8388864 | tf_op jit(solution)/shard_map/jit(_where)/select_n | solution.py:94
  340.4 6.3 %copy.53 = bf16[256,8192]{1,0:T(8,128)(2,1)} copy(bf16[256,8192]{0,1:T(8,128)(2,1)} %bitcast_select_fusion.1) | data formatting | bytes 8388608 | tf_op jit(solution)/shard_map/jit(_where)/select_n | solution.py:94
  (73 shorter events, 61.4 us)
Async XLA Ops:
  0.7 18.0 %collective-permute-start.19 = (s32[128]{0:T(128)S(1)}, s32[128]{0:T(128)S(1)}, u32[]{:S(2)}, u32[]{:S(2)}) collective-permute-start(s32[128]{0:T(128)S(1)} %broadcast_add_fusion), channel_id=1, source_target_pairs={{0,4},{1,5},{2,6},{3,7},{4,8},{5,9},{6,10},{7,11},{8,12},{9,13},{1... | collective-permute-start | bytes 1544 | tf_op jit(solution)/shard_map/ppermute | solution.py:16
  3.9 16.8 %collective-permute-start.20 = (s32[128]{0:T(128)S(1)}, s32[128]{0:T(128)S(1)}, u32[]{:S(2)}, u32[]{:S(2)}) collective-permute-start(s32[128]{0:T(128)S(1)} %broadcast_add_fusion), channel_id=1, source_target_pairs={{0,3},{1,4},{2,5},{3,6},{4,7},{5,8},{6,9},{7,10},{8,11},{9,12},{10... | collective-permute-start | bytes 1544 | tf_op jit(solution)/shard_map/ppermute | solution.py:16
  8.0 14.7 %collective-permute-start.21 = (s32[128]{0:T(128)S(1)}, s32[128]{0:T(128)S(1)}, u32[]{:S(2)}, u32[]{:S(2)}) collective-permute-start(s32[128]{0:T(128)S(1)} %broadcast_add_fusion), channel_id=1, source_target_pairs={{0,2},{1,3},{2,4},{3,5},{4,6},{5,7},{6,8},{7,9},{8,10},{9,11},{10,... | collective-permute-start | bytes 1544 | tf_op jit(solution)/shard_map/ppermute | solution.py:16
  9.9 15.0 %collective-permute-start.22 = (s32[128]{0:T(128)S(1)}, s32[128]{0:T(128)S(1)}, u32[]{:S(2)}, u32[]{:S(2)}) collective-permute-start(s32[128]{0:T(128)S(1)} %broadcast_add_fusion), channel_id=1, source_target_pairs={{0,1},{1,2},{2,3},{3,4},{4,5},{5,6},{6,7},{7,8},{8,9},{9,10},{10,1... | collective-permute-start | bytes 1544 | tf_op jit(solution)/shard_map/ppermute | solution.py:16
  14.6 15.8 %collective-permute-start.15 = (bf16[128,2048]{0,1:T(8,128)(2,1)S(1)}, bf16[128,2048]{0,1:T(8,128)(2,1)S(1)}, u32[]{:S(2)}, u32[]{:S(2)}) collective-permute-start(bf16[128,2048]{0,1:T(8,128)(2,1)S(1)} %copy.41), channel_id=1, source_target_pairs={{0,4},{1,5},{2,6},{3,7},{4,8},{5,9},{6,10},{7,11},{8,12},{9,13},{1... | collective-permute-start | bytes 1572872 | tf_op jit(solution)/shard_map/ppermute | solution.py:16
  18.8 20.7 %collective-permute-start.16 = (bf16[128,2048]{0,1:T(8,128)(2,1)S(1)}, bf16[128,2048]{0,1:T(8,128)(2,1)S(1)}, u32[]{:S(2)}, u32[]{:S(2)}) collective-permute-start(bf16[128,2048]{0,1:T(8,128)(2,1)S(1)} %copy.41), channel_id=1, source_target_pairs={{0,3},{1,4},{2,5},{3,6},{4,7},{5,8},{6,9},{7,10},{8,11},{9,12},{10... | collective-permute-start | bytes 1572872 | tf_op jit(solution)/shard_map/ppermute | solution.py:16
  20.7 29.8 %collective-permute-start.17 = (bf16[128,2048]{0,1:T(8,128)(2,1)S(1)}, bf16[128,2048]{0,1:T(8,128)(2,1)S(1)}, u32[]{:S(2)}, u32[]{:S(2)}) collective-permute-start(bf16[128,2048]{0,1:T(8,128)(2,1)S(1)} %copy.41), channel_id=1, source_target_pairs={{0,2},{1,3},{2,4},{3,5},{4,6},{5,7},{6,8},{7,9},{8,10},{9,11},{10,... | collective-permute-start | bytes 1572872 | tf_op jit(solution)/shard_map/ppermute | solution.py:16
  22.7 33.4 %collective-permute-start.18 = (bf16[128,2048]{0,1:T(8,128)(2,1)S(1)}, bf16[128,2048]{0,1:T(8,128)(2,1)S(1)}, u32[]{:S(2)}, u32[]{:S(2)}) collective-permute-start(bf16[128,2048]{0,1:T(8,128)(2,1)S(1)} %copy.41), channel_id=1, source_target_pairs={{0,1},{1,2},{2,3},{3,4},{4,5},{5,6},{6,7},{7,8},{8,9},{9,10},{10,1... | collective-permute-start | bytes 1572872 | tf_op jit(solution)/shard_map/ppermute | solution.py:16
  77.3 107.3 %all-to-all-start = ((bf16[128,16,512]{0,2,1:T(8,128)(2,1)}), bf16[128,16,512]{0,2,1:T(8,128)(2,1)S(1)}, u32[]{:S(2)}, u32[]{:S(2)}) async-start(bf16[128,16,512]{0,2,1:T(8,128)(2,1)} %bitcast.71), calls=%async_computation | async-start | bytes 4194304 | tf_op jit(solution)/shard_map/all_to_all | solution.py:89
  84.2 45.1 %collective-permute-start = (s32[1,2]{0,1:T(2,128)S(1)}, s32[1,2]{0,1:T(2,128)S(1)}, u32[]{:S(2)}, u32[]{:S(2)}) collective-permute-start(s32[1,2]{0,1:T(2,128)S(1)} %copy.37), channel_id=1, source_target_pairs={{0,1},{1,2},{2,3},{3,4},{4,5},{5,6},{6,7},{7,8},{8,9},{9,10},{10,1... | collective-permute-start | bytes 32 | tf_op jit(solution)/shard_map/ppermute | solution.py:79
  129.3 4.0 %collective-permute-start.1 = (s32[1,2]{0,1:T(2,128)S(1)}, s32[1,2]{0,1:T(2,128)S(1)}, u32[]{:S(2)}, u32[]{:S(2)}) collective-permute-start(s32[1,2]{0,1:T(2,128)S(1)} %collective-permute-done), channel_id=1, source_target_pairs={{0,1},{1,2},{2,3},{3,4},{4,5},{5,6},{6,7},{7,8},{8,9},{9,10},{10,1... | collective-permute-start | bytes 32 | tf_op jit(solution)/shard_map/ppermute | solution.py:79
  133.3 3.9 %collective-permute-start.2 = (s32[1,2]{0,1:T(2,128)S(1)}, s32[1,2]{0,1:T(2,128)S(1)}, u32[]{:S(2)}, u32[]{:S(2)}) collective-permute-start(s32[1,2]{0,1:T(2,128)S(1)} %collective-permute-done.1), channel_id=1, source_target_pairs={{0,1},{1,2},{2,3},{3,4},{4,5},{5,6},{6,7},{7,8},{8,9},{9,10},{10,1... | collective-permute-start | bytes 32 | tf_op jit(solution)/shard_map/ppermute | solution.py:79
  137.2 3.9 %collective-permute-start.3 = (s32[1,2]{0,1:T(2,128)S(1)}, s32[1,2]{0,1:T(2,128)S(1)}, u32[]{:S(2)}, u32[]{:S(2)}) collective-permute-start(s32[1,2]{0,1:T(2,128)S(1)} %collective-permute-done.2), channel_id=1, source_target_pairs={{0,1},{1,2},{2,3},{3,4},{4,5},{5,6},{6,7},{7,8},{8,9},{9,10},{10,1... | collective-permute-start | bytes 32 | tf_op jit(solution)/shard_map/ppermute | solution.py:79
  141.1 3.9 %collective-permute-start.4 = (s32[1,2]{0,1:T(2,128)S(1)}, s32[1,2]{0,1:T(2,128)S(1)}, u32[]{:S(2)}, u32[]{:S(2)}) collective-permute-start(s32[1,2]{0,1:T(2,128)S(1)} %collective-permute-done.3), channel_id=1, source_target_pairs={{0,1},{1,2},{2,3},{3,4},{4,5},{5,6},{6,7},{7,8},{8,9},{9,10},{10,1... | collective-permute-start | bytes 32 | tf_op jit(solution)/shard_map/ppermute | solution.py:79
  145.0 3.9 %collective-permute-start.5 = (s32[1,2]{0,1:T(2,128)S(1)}, s32[1,2]{0,1:T(2,128)S(1)}, u32[]{:S(2)}, u32[]{:S(2)}) collective-permute-start(s32[1,2]{0,1:T(2,128)S(1)} %collective-permute-done.4), channel_id=1, source_target_pairs={{0,1},{1,2},{2,3},{3,4},{4,5},{5,6},{6,7},{7,8},{8,9},{9,10},{10,1... | collective-permute-start | bytes 32 | tf_op jit(solution)/shard_map/ppermute | solution.py:79
  148.9 3.9 %collective-permute-start.6 = (s32[1,2]{0,1:T(2,128)S(1)}, s32[1,2]{0,1:T(2,128)S(1)}, u32[]{:S(2)}, u32[]{:S(2)}) collective-permute-start(s32[1,2]{0,1:T(2,128)S(1)} %collective-permute-done.5), channel_id=1, source_target_pairs={{0,1},{1,2},{2,3},{3,4},{4,5},{5,6},{6,7},{7,8},{8,9},{9,10},{10,1... | collective-permute-start | bytes 32 | tf_op jit(solution)/shard_map/ppermute | solution.py:79
  152.8 3.9 %collective-permute-start.7 = (s32[1,2]{0,1:T(2,128)S(1)}, s32[1,2]{0,1:T(2,128)S(1)}, u32[]{:S(2)}, u32[]{:S(2)}) collective-permute-start(s32[1,2]{0,1:T(2,128)S(1)} %collective-permute-done.6), channel_id=1, source_target_pairs={{0,1},{1,2},{2,3},{3,4},{4,5},{5,6},{6,7},{7,8},{8,9},{9,10},{10,1... | collective-permute-start | bytes 32 | tf_op jit(solution)/shard_map/ppermute | solution.py:79
  156.7 3.9 %collective-permute-start.8 = (s32[1,2]{0,1:T(2,128)S(1)}, s32[1,2]{0,1:T(2,128)S(1)}, u32[]{:S(2)}, u32[]{:S(2)}) collective-permute-start(s32[1,2]{0,1:T(2,128)S(1)} %collective-permute-done.7), channel_id=1, source_target_pairs={{0,1},{1,2},{2,3},{3,4},{4,5},{5,6},{6,7},{7,8},{8,9},{9,10},{10,1... | collective-permute-start | bytes 32 | tf_op jit(solution)/shard_map/ppermute | solution.py:79
  160.6 3.9 %collective-permute-start.9 = (s32[1,2]{0,1:T(2,128)S(1)}, s32[1,2]{0,1:T(2,128)S(1)}, u32[]{:S(2)}, u32[]{:S(2)}) collective-permute-start(s32[1,2]{0,1:T(2,128)S(1)} %collective-permute-done.8), channel_id=1, source_target_pairs={{0,1},{1,2},{2,3},{3,4},{4,5},{5,6},{6,7},{7,8},{8,9},{9,10},{10,1... | collective-permute-start | bytes 32 | tf_op jit(solution)/shard_map/ppermute | solution.py:79
  164.5 3.9 %collective-permute-start.10 = (s32[1,2]{0,1:T(2,128)S(1)}, s32[1,2]{0,1:T(2,128)S(1)}, u32[]{:S(2)}, u32[]{:S(2)}) collective-permute-start(s32[1,2]{0,1:T(2,128)S(1)} %collective-permute-done.9), channel_id=1, source_target_pairs={{0,1},{1,2},{2,3},{3,4},{4,5},{5,6},{6,7},{7,8},{8,9},{9,10},{10,1... | collective-permute-start | bytes 32 | tf_op jit(solution)/shard_map/ppermute | solution.py:79
  168.4 3.9 %collective-permute-start.11 = (s32[1,2]{0,1:T(2,128)S(1)}, s32[1,2]{0,1:T(2,128)S(1)}, u32[]{:S(2)}, u32[]{:S(2)}) collective-permute-start(s32[1,2]{0,1:T(2,128)S(1)} %collective-permute-done.10), channel_id=1, source_target_pairs={{0,1},{1,2},{2,3},{3,4},{4,5},{5,6},{6,7},{7,8},{8,9},{9,10},{10,1... | collective-permute-start | bytes 32 | tf_op jit(solution)/shard_map/ppermute | solution.py:79
  172.3 3.9 %collective-permute-start.12 = (s32[1,2]{0,1:T(2,128)S(1)}, s32[1,2]{0,1:T(2,128)S(1)}, u32[]{:S(2)}, u32[]{:S(2)}) collective-permute-start(s32[1,2]{0,1:T(2,128)S(1)} %collective-permute-done.11), channel_id=1, source_target_pairs={{0,1},{1,2},{2,3},{3,4},{4,5},{5,6},{6,7},{7,8},{8,9},{9,10},{10,1... | collective-permute-start | bytes 32 | tf_op jit(solution)/shard_map/ppermute | solution.py:79
  180.1 3.9 %collective-permute-start.14 = (s32[1,2]{0,1:T(2,128)S(1)}, s32[1,2]{0,1:T(2,128)S(1)}, u32[]{:S(2)}, u32[]{:S(2)}) collective-permute-start(s32[1,2]{0,1:T(2,128)S(1)} %collective-permute-done.13), channel_id=1, source_target_pairs={{0,1},{1,2},{2,3},{3,4},{4,5},{5,6},{6,7},{7,8},{8,9},{9,10},{10,1... | collective-permute-start | bytes 32 | tf_op jit(solution)/shard_map/ppermute | solution.py:79
  213.6 116.0 %all-to-all-start.1 = ((bf16[256,16,512]{2,0,1:T(8,128)(2,1)}), bf16[256,16,512]{2,0,1:T(8,128)(2,1)}, u32[]{:S(2)}, u32[]{:S(2)}) async-start(bf16[256,16,512]{2,0,1:T(8,128)(2,1)} %copy_select_fusion), calls=%async_computation.1 | async-start | bytes 8388608 | tf_op jit(solution)/shard_map/all_to_all | solution.py:39
  (6 other events, 77.1 us)
